TPU v7x, 32 devices: a whole 2x2x4 slice. The times are simulated.
32 devices in a mesh: row: 16 (over z, y, x), col: 2 (over core).
Axes of the slice: x: 2, y: 2, z: 4, core: 2. Of those that a mesh axis runs over, the one named last changes fastest.
Arguments:
- sim_points: float32 [64, 4096], P(None, 'row'), may hold values from -34 to 34
- obs_points: float32 [64, 4096], P(None, ('row', 'col')), may hold values from -16 to 16
- sim_logw: float32 [4096], P('row'), may hold values from -2.5 to 2.5
- obs_logw: float32 [4096], P(('row', 'col')), may hold values from -2.5 to 2.5
Outputs:
- potential_f: float32 [4096], P('row')
- potential_g: float32 [4096], P(('row', 'col'))
- transport_cost: float32 [1], replicated
All inputs are finite; a program needn't handle non-finite values.
Results may differ from a plain program's by a relative error of at most 0.0003.
Values sent between devices are 32-bit elements; how exact they have to be, the bound alone decides.
A program may use at most 64 MiB of HBM per device.

v0:
```python
import math

import jax
import jax.numpy as jnp
from jax import lax
from jax.sharding import PartitionSpec as P

ITERS = 8


epsilon = 0.05


def joined(value, axis, join):
    pieces = jax.tree.map(lambda part: lax.all_gather(part, axis), value)
    head = jax.tree.map(lambda part: part[0], pieces)
    tail = jax.tree.map(lambda part: part[1:], pieces)
    total, _ = lax.scan(lambda total, piece: (join(total, piece), None), head, tail)
    return total


def pair_cost(points, observed):
    feature_count = points.shape[0]
    sq_points = jnp.sum(points * points, 0)
    sq_observed = jnp.sum(observed * observed, 0)
    inner_products = lax.dot_general(
        points,
        observed,
        (((0,), (0,)), ((), ())),
        precision=lax.Precision.HIGHEST,
        preferred_element_type=jnp.float32,
    )
    return (sq_points[:, None] + sq_observed[None, :] - 2.0 * inner_products) / feature_count


def lse_combine(first, second):
    new_top = jnp.maximum(first[0], second[0])
    return (
        new_top,
        first[1] * jnp.exp(first[0] - new_top) + second[1] * jnp.exp(second[0] - new_top),
    )


def on_device(sim_points, obs_points, sim_logw, obs_logw):
    row_count = lax.axis_size("row")
    obs_dev = obs_points.shape[1]
    total_sim = sim_points.shape[1] * row_count
    total_obs = obs_dev * row_count * lax.axis_size("col")
    observed, logw_all = (
        lax.all_gather(obs_points, "row", axis=1, tiled=True),
        lax.all_gather(obs_logw, "row", axis=0, tiled=True),
    )
    log_a = sim_logw - math.log(total_sim)
    log_b_all = logw_all - math.log(total_obs)
    own_index = lax.axis_index("row")
    resident = pair_cost(sim_points, observed)

    def costs():
        return resident

    potential_g = jnp.zeros((observed.shape[1],), jnp.float32)
    potential_g_own = jnp.zeros((obs_dev,), jnp.float32)
    potential_f = jnp.zeros((sim_points.shape[1],), jnp.float32)
    for iteration in range(ITERS):
        scores = (potential_g[None, :] - costs()) / epsilon
        row_top = jnp.max(scores, 1)
        row_mass = jnp.sum(jnp.exp(scores - row_top[:, None]), 1)
        row_top, row_mass = joined((row_top, row_mass), "col", lse_combine)
        potential_f = epsilon * log_a - epsilon * (row_top + jnp.log(row_mass))
        scores = (potential_f[:, None] - costs()) / epsilon
        col_top = jnp.max(scores, 0)
        col_mass = jnp.sum(jnp.exp(scores - col_top[None, :]), 0)
        col_top, col_mass = joined((col_top, col_mass), "row", lse_combine)
        potential_g = epsilon * log_b_all - epsilon * (col_top + jnp.log(col_mass))
        potential_g_own = lax.dynamic_slice_in_dim(potential_g, own_index * obs_dev, obs_dev)
    costs_tile = costs()
    transport = jnp.exp((potential_f[:, None] + potential_g[None, :] - costs_tile) / epsilon)
    total_cost = lax.psum(jnp.sum(transport * costs_tile), ("row", "col"))
    return (potential_f, potential_g_own, jnp.reshape(total_cost, (1,)))


def solution(mesh):
    in_specs = (P(None, "row"), P(None, ("row", "col")), P("row"), P(("row", "col")))
    out_specs = (P("row"), P(("row", "col")), P())
    return jax.shard_map(
        on_device, mesh=mesh, in_specs=in_specs, out_specs=out_specs, check_vma=False
    )
```

profile of v0, /device:TPU:0, one launch (start us, length us, event | category | flops | bytes accessed | tf_op | source)
XLA Modules:
  0.0 769.4 jit_solution(11684991094862416299)
XLA Ops:
  0.6 45.6 %all_gather.199 = f32[64,2048]{1,0:T(8,128)S(1)} all-gather(f32[64,128]{1,0:T(8,128)} %param.21), channel_id=1, replica_groups=mesh['row'=16,'col'=2] {'row'}, dimensions={1}, use_global_device_ids=true | all-gather | bytes 557056 | tf_op jit(solution)/shard_map/all_gather | solution.py:50
  47.1 3.2 fusion.2
  50.3 35.3 %all-gather.32 = f32[16,1,128]{2,1,0:T(1,128)S(1)} all-gather(f32[1,1,128]{2,1,0:T(1,128)S(1)} %bitcast.173), channel_id=1, replica_groups=mesh['row'=16,'col'=2] {'row'}, dimensions={0}, use_global_device_ids=true | all-gather | bytes 8704 | tf_op jit(solution)/shard_map/all_gather | solution.py:51
  90.0 38.2 %all-gather.2 = f32[32768]{0:T(1024)S(1)} all-gather(f32[2048]{0:T(1024)S(1)} %fusion.3), channel_id=4, replica_groups=mesh['row'=16,'col'=2] {'row'}, dimensions={0}, use_global_device_ids=true | all-gather | bytes 139264 | tf_op jit(solution)/shard_map/all_gather | solution.py:15
  128.6 36.1 %all-gather.3 = f32[32768]{0:T(1024)S(1)} all-gather(f32[2048]{0:T(1024)S(1)} %exponential_reduce_fusion.14), channel_id=5, replica_groups=mesh['row'=16,'col'=2] {'row'}, dimensions={0}, use_global_device_ids=true | all-gather | bytes 139264 | tf_op jit(solution)/shard_map/all_gather | solution.py:15
  166.7 1.8 all-gather.36
  170.5 38.2 %all-gather.6 = f32[32768]{0:T(1024)S(1)} all-gather(f32[2048]{0:T(1024)S(1)} %fusion.5), channel_id=8, replica_groups=mesh['row'=16,'col'=2] {'row'}, dimensions={0}, use_global_device_ids=true | all-gather | bytes 139264 | tf_op jit(solution)/shard_map/all_gather | solution.py:15
  209.2 36.1 %all-gather.7 = f32[32768]{0:T(1024)S(1)} all-gather(f32[2048]{0:T(1024)S(1)} %exponential_reduce_fusion.12), channel_id=9, replica_groups=mesh['row'=16,'col'=2] {'row'}, dimensions={0}, use_global_device_ids=true | all-gather | bytes 139264 | tf_op jit(solution)/shard_map/all_gather | solution.py:15
  247.2 1.8 all-gather.38
  251.1 38.2 %all-gather.10 = f32[32768]{0:T(1024)S(1)} all-gather(f32[2048]{0:T(1024)S(1)} %fusion.7), channel_id=12, replica_groups=mesh['row'=16,'col'=2] {'row'}, dimensions={0}, use_global_device_ids=true | all-gather | bytes 139264 | tf_op jit(solution)/shard_map/all_gather | solution.py:15
  289.8 36.1 %all-gather.11 = f32[32768]{0:T(1024)S(1)} all-gather(f32[2048]{0:T(1024)S(1)} %exponential_reduce_fusion.10), channel_id=13, replica_groups=mesh['row'=16,'col'=2] {'row'}, dimensions={0}, use_global_device_ids=true | all-gather | bytes 139264 | tf_op jit(solution)/shard_map/all_gather | solution.py:15
  327.8 1.8 all-gather.40
  331.7 38.2 %all-gather.14 = f32[32768]{0:T(1024)S(1)} all-gather(f32[2048]{0:T(1024)S(1)} %fusion.9), channel_id=16, replica_groups=mesh['row'=16,'col'=2] {'row'}, dimensions={0}, use_global_device_ids=true | all-gather | bytes 139264 | tf_op jit(solution)/shard_map/all_gather | solution.py:15
  370.3 36.1 %all-gather.15 = f32[32768]{0:T(1024)S(1)} all-gather(f32[2048]{0:T(1024)S(1)} %exponential_reduce_fusion.8), channel_id=17, replica_groups=mesh['row'=16,'col'=2] {'row'}, dimensions={0}, use_global_device_ids=true | all-gather | bytes 139264 | tf_op jit(solution)/shard_map/all_gather | solution.py:15
  412.2 38.2 %all-gather.18 = f32[32768]{0:T(1024)S(1)} all-gather(f32[2048]{0:T(1024)S(1)} %fusion.11), channel_id=20, replica_groups=mesh['row'=16,'col'=2] {'row'}, dimensions={0}, use_global_device_ids=true | all-gather | bytes 139264 | tf_op jit(solution)/shard_map/all_gather | solution.py:15
  450.9 36.4 %all-gather.19 = f32[32768]{0:T(1024)S(1)} all-gather(f32[2048]{0:T(1024)S(1)} %exponential_reduce_fusion.6), channel_id=21, replica_groups=mesh['row'=16,'col'=2] {'row'}, dimensions={0}, use_global_device_ids=true | all-gather | bytes 139264 | tf_op jit(solution)/shard_map/all_gather | solution.py:15
  493.1 38.0 %all-gather.22 = f32[32768]{0:T(1024)S(1)} all-gather(f32[2048]{0:T(1024)S(1)} %fusion.13), channel_id=24, replica_groups=mesh['row'=16,'col'=2] {'row'}, dimensions={0}, use_global_device_ids=true | all-gather | bytes 139264 | tf_op jit(solution)/shard_map/all_gather | solution.py:15
  531.6 36.3 %all-gather.23 = f32[32768]{0:T(1024)S(1)} all-gather(f32[2048]{0:T(1024)S(1)} %exponential_reduce_fusion.4), channel_id=25, replica_groups=mesh['row'=16,'col'=2] {'row'}, dimensions={0}, use_global_device_ids=true | all-gather | bytes 139264 | tf_op jit(solution)/shard_map/all_gather | solution.py:15
  573.7 38.0 %all-gather.26 = f32[32768]{0:T(1024)S(1)} all-gather(f32[2048]{0:T(1024)S(1)} %fusion.15), channel_id=28, replica_groups=mesh['row'=16,'col'=2] {'row'}, dimensions={0}, use_global_device_ids=true | all-gather | bytes 139264 | tf_op jit(solution)/shard_map/all_gather | solution.py:15
  612.2 36.3 %all-gather.27 = f32[32768]{0:T(1024)S(1)} all-gather(f32[2048]{0:T(1024)S(1)} %exponential_reduce_fusion.2), channel_id=29, replica_groups=mesh['row'=16,'col'=2] {'row'}, dimensions={0}, use_global_device_ids=true | all-gather | bytes 139264 | tf_op jit(solution)/shard_map/all_gather | solution.py:15
  650.4 1.8 all-gather.48
  654.2 38.0 %all-gather.30 = f32[32768]{0:T(1024)S(1)} all-gather(f32[2048]{0:T(1024)S(1)} %fusion.17), channel_id=32, replica_groups=mesh['row'=16,'col'=2] {'row'}, dimensions={0}, use_global_device_ids=true | all-gather | bytes 139264 | tf_op jit(solution)/shard_map/all_gather | solution.py:15
  692.8 36.3 %all-gather.31 = f32[32768]{0:T(1024)S(1)} all-gather(f32[2048]{0:T(1024)S(1)} %exponential_reduce_fusion), channel_id=33, replica_groups=mesh['row'=16,'col'=2] {'row'}, dimensions={0}, use_global_device_ids=true | all-gather | bytes 139264 | tf_op jit(solution)/shard_map/all_gather | solution.py:15
  732.3 37.1 %psum.7 = f32[1]{0:T(128)} all-reduce(f32[1]{0:T(128)} %bitcast.66), channel_id=1, replica_groups=mesh['row'=16,'col'=2] {'row','col'}, use_global_device_ids=true, to_apply=%region_51.52 | all-reduce | flops 1 | bytes 8 | tf_op jit(solution)/shard_map/psum | solution.py:78
  (382 shorter events, 49.3 us)
Async XLA Ops:
  46.2 4.1 copy-start.2
  47.1 42.5 %copy-start = (f32[256]{0:T(256)S(1)}, f32[256]{0:T(256)}, u32[]{:S(2)}) copy-start(f32[256]{0:T(256)} %param.22) | copy-start | bytes 3076
  653.9 76.8 %copy-start.1 = (f32[256]{0:T(256)}, f32[256]{0:T(256)S(1)}, u32[]{:S(2)}) copy-start(f32[256]{0:T(256)S(1)} %multiply_subtract_fusion.8) | copy-start | bytes 3076
where the time goes:
time: 771 us; the launch traced here: 769 us
  blocking collectives  741 us (96%)
  other arithmetic  17 us (2%)
    all_gather x32, blocking collectives, joined(): pieces = jax.tree.map(lambda part: lax.all_gather(part, axis), value)  623 us
    all_gather x1, blocking collectives, on_device(): lax.all_gather(obs_points, 'row', axis=1, tiled=True)  45.6 us
    psum x1, blocking collectives, on_device(): total_cost = lax.psum(jnp.sum(transport * costs_tile), ('row', 'col'))  37.1 us
    all_gather x1, blocking collectives, on_device(): lax.all_gather(obs_logw, 'row', axis=0, tiled=True)  35.3 us

commit v1 on v0

v1 whole, which is shorter than its diff:
```python
import functools
import math

import jax
import jax.numpy as jnp
from jax import lax
from jax.experimental import pallas as pl
from jax.experimental.pallas import tpu as pltpu

ITERS = 8
EPSILON = 0.05
LOG2E = 1.0 / math.log(2.0)
PLANE = 4
REBUILD = 3
LIFT = 60.0
MESH = pl.DeviceIdType.MESH
PARTS = 2


def split_rows(row):
    high = row.astype(jnp.bfloat16).astype(jnp.float32)
    rest = row - high
    middle = rest.astype(jnp.bfloat16).astype(jnp.float32)
    low = rest - middle
    shape = (16, row.shape[1])
    index = lax.broadcasted_iota(jnp.int32, shape, 0)
    full = lambda part: jnp.broadcast_to(part, shape)
    rows = jnp.where(
        index == 0,
        full(high),
        jnp.where(index == 1, full(middle), jnp.where(index == 2, full(low), 0.0)),
    )
    return rows.astype(jnp.bfloat16)


def matvec(rows, parts, contract):
    total = None
    for part in parts:
        out = lax.dot_general(
            rows, part[...], (((1,), (contract,)), ((), ())), preferred_element_type=jnp.float32
        )
        total = out if total is None else total + out
    return total[0:1] + total[1:2] + total[2:3]


def to_column(row):
    return jnp.broadcast_to(row, (128, row.shape[1])).T


def to_row(column):
    return jnp.broadcast_to(column, (column.shape[0], 128)).T[0:1]


def body(
    rows_n, cols_n, plane,
    sim_ref, obs_ref, slw_ref, olw_ref,
    f_ref, g_ref, cost_ref,
    simg, obsg, d_ref, k_ref, x_ref,
    row_first, col_first, row_buf, col_buf, end_buf,
    send_sem, recv_sem,
):
    lines = rows_n // plane
    width, n_sim = sim_ref.shape
    n_obs = obs_ref.shape[1]
    n_i = plane * n_sim
    n_j = lines * n_obs
    r = lax.axis_index("row")
    c = lax.axis_index("col")
    z = r // plane
    q = r % plane
    group = plane * cols_n
    me = q * cols_n + c

    plane_peers = []
    for step in range(1, group):
        other = (me + step) % group
        plane_peers.append((z * plane + other // cols_n, other % cols_n))
    line_peers = []
    for step in range(1, lines):
        line_peers.append((((z + step) % lines) * plane + q, c))
    core_peers = []
    for step in range(1, plane):
        core_peers.append((z * plane + (q + step) % plane, c))

    barrier = pltpu.get_barrier_semaphore()
    for peer in plane_peers + line_peers:
        pl.semaphore_signal(barrier, inc=1, device_id=peer, device_id_type=MESH)

    scale = LOG2E / (EPSILON * width)
    x = sim_ref[...]
    y = obs_ref[...]
    pad = simg.shape[1] - width

    def tail(values, n):
        index = lax.broadcasted_iota(jnp.int32, (pad, n), 0)
        out = jnp.zeros((pad, n), jnp.float32)
        for k, value in enumerate(values):
            if value is not None:
                out = jnp.where(index == k, jnp.broadcast_to(value, (pad, n)), out)
        return out

    one = jnp.ones((1, n_sim), jnp.float32)
    simg[q, :width, :] = x
    simg[q, width:, :] = tail(
        [jnp.sum(x * x, 0, keepdims=True), one, slw_ref[...]], n_sim
    )
    ones_obs = jnp.full((1, n_obs), scale, jnp.float32)
    obsg[z, :width, :] = y * (-2.0 * scale)
    obsg[z, width:, :] = tail(
        [ones_obs, jnp.sum(y * y, 0, keepdims=True) * scale, None, olw_ref[...]], n_obs
    )
    pl.semaphore_wait(barrier, len(plane_peers) + len(line_peers))

    def exchange(buf, own, peers, sem):
        for peer in peers:
            pltpu.make_async_remote_copy(
                src_ref=buf.at[own], dst_ref=buf.at[own],
                send_sem=send_sem.at[sem], recv_sem=recv_sem.at[sem],
                device_id=peer, device_id_type=MESH,
            ).start()

    def finish(buf, peers, sem):
        if peers:
            some = buf.at[pl.ds(0, len(peers))]
            pltpu.make_async_copy(some, some, recv_sem.at[sem]).wait()
            pltpu.make_async_copy(some, some, send_sem.at[sem]).wait()

    exchange(obsg, z, line_peers, 0)
    exchange(simg, q, core_peers, 1)
    finish(obsg, line_peers, 0)
    finish(simg, core_peers, 1)

    log_a = jnp.concatenate(
        [simg[k, width + 2:width + 3, :] for k in range(plane)], axis=1
    ) * LOG2E - math.log2(n_sim * rows_n)
    log_b = jnp.concatenate(
        [obsg[k, width + 3:width + 4, :] for k in range(lines)], axis=1
    ) * LOG2E - math.log2(n_obs * rows_n * cols_n)

    for k in range(lines):
        left = obsg[k].T
        for m in range(plane):
            d_ref[k * n_obs:(k + 1) * n_obs, m * n_sim:(m + 1) * n_sim] = lax.dot_general(
                left, simg[m], (((1,), (0,)), ((), ())),
                precision=lax.Precision.HIGHEST, preferred_element_type=jnp.float32,
            )

    d = d_ref[...]
    low = jnp.min(d, 0, keepdims=True)
    mass = jnp.sum(jnp.exp2(low - d), 0, keepdims=True)
    row_first[me, 0:1, :] = low
    row_first[me, 1:2, :] = mass
    exchange(row_first, me, plane_peers, 2)
    finish(row_first, plane_peers, 2)

    def merge(buf, count):
        low = buf[0, 0:1, :]
        for k in range(1, count):
            low = jnp.minimum(low, buf[k, 0:1, :])
        mass = buf[0, 1:2, :] * jnp.exp2(low - buf[0, 0:1, :])
        for k in range(1, count):
            mass = mass + buf[k, 1:2, :] * jnp.exp2(low - buf[k, 0:1, :])
        return low - jnp.log2(mass)

    f = log_a + merge(row_first, group)
    scores = d_ref[...] - f
    low = jnp.min(scores, 1, keepdims=True)
    mass = jnp.sum(jnp.exp2(low - scores), 1, keepdims=True)
    col_first[z, 0:1, :] = to_row(low)
    col_first[z, 1:2, :] = to_row(mass)
    exchange(col_first, z, line_peers, 3)
    finish(col_first, line_peers, 3)
    g = log_b + merge(col_first, lines)

    a_lifted = jnp.exp2(log_a + LIFT)
    b_lifted = jnp.exp2(log_b + LIFT)

    def store_parts(ref, value, rows):
        high = value.astype(jnp.bfloat16)
        ref[0, rows, :] = high
        if PARTS > 1:
            ref[1, rows, :] = (value - high.astype(jnp.float32)).astype(jnp.bfloat16)

    def build(f, g, with_cost):
        column = to_column(g + LIFT)
        for j in range(0, n_j, 64):
            rows = pl.ds(j, 64)
            piece = column[j:j + 64]
            shift = jnp.concatenate([piece] * (n_i // 128), axis=1)
            values = jnp.exp2((f + shift) - d_ref[rows, :])
            store_parts(k_ref, values, rows)
            if with_cost:
                store_parts(x_ref, values * d_ref[rows, :], rows)

    def total_of(buf, count):
        total = buf[0, 0:1, :]
        for k in range(1, count):
            total = total + buf[k, 0:1, :]
        return total

    def row_half(v_rows, parity):
        buf = row_buf.at[parity]
        buf[me, 0:1, :] = matvec(v_rows, [k_ref.at[p] for p in range(PARTS)], 0)
        exchange(buf, me, plane_peers, 4 + parity)
        finish(buf, plane_peers, 4 + parity)
        return a_lifted / total_of(buf, group)

    def col_half(u, parity):
        buf = col_buf.at[parity]
        buf[z, 0:1, :] = matvec(split_rows(u), [k_ref.at[p] for p in range(PARTS)], 1)
        exchange(buf, z, line_peers, 6 + parity)
        finish(buf, line_peers, 6 + parity)
        return b_lifted / total_of(buf, lines)

    done = 1
    while done < ITERS - 1:
        count = min(REBUILD, ITERS - 1 - done)
        build(f, g, False)

        def step(iteration, carry):
            _, v = carry
            parity = iteration % 2
            u = row_half(split_rows(v), parity)
            return u, col_half(u, parity)

        u, v = lax.fori_loop(
            done, done + count, step,
            (jnp.ones((1, n_i), jnp.float32), jnp.ones((1, n_j), jnp.float32)),
        )
        f = f + jnp.log2(u)
        g = g + jnp.log2(v)
        done += count

    build(f, g, True)
    parity = (ITERS - 1) % 2
    u = row_half(split_rows(jnp.ones((1, n_j), jnp.float32)), parity)
    u_rows = split_rows(u)
    col_first[z, 0:1, :] = matvec(u_rows, [k_ref.at[p] for p in range(PARTS)], 1)
    col_first[z, 1:2, :] = matvec(u_rows, [x_ref.at[p] for p in range(PARTS)], 1)
    exchange(col_first, z, line_peers, 3)
    f = f + jnp.log2(u)
    f_mine = f[:, 0:n_sim]
    for k in range(1, plane):
        f_mine = jnp.where(q == k, f[:, k * n_sim:(k + 1) * n_sim], f_mine)
    f_ref[...] = f_mine * (EPSILON / LOG2E)
    finish(col_first, line_peers, 3)
    sums = col_first[0]
    for k in range(1, lines):
        sums = sums + col_first[k]
    v = b_lifted / sums[0:1]
    share = jnp.sum(v * 2.0 ** -LIFT * sums[1:2], axis=1, keepdims=True)
    end_buf[me] = jnp.broadcast_to(share * (EPSILON / LOG2E), (1, 128))
    exchange(end_buf, me, plane_peers, 8)
    g = g + jnp.log2(v)
    g_mine = g[:, 0:n_obs]
    for k in range(1, lines):
        g_mine = jnp.where(z == k, g[:, k * n_obs:(k + 1) * n_obs], g_mine)
    g_ref[...] = g_mine * (EPSILON / LOG2E)
    finish(end_buf, plane_peers, 8)
    cost_ref[...] = total_of(end_buf, group)[:, 0:1]


def on_device(sizes, sim_points, obs_points, sim_logw, obs_logw):
    rows_n, cols_n = sizes
    plane = math.gcd(PLANE, rows_n)
    lines = rows_n // plane
    group = plane * cols_n
    width, n_sim = sim_points.shape
    n_obs = obs_points.shape[1]
    n_i, n_j = plane * n_sim, lines * n_obs
    f32, bf16 = jnp.float32, jnp.bfloat16
    depth = -(-width // 8) * 8 + 8
    assert width % 8 == 0
    vmem = pl.BlockSpec(memory_space=pltpu.VMEM)
    f, g, cost = pl.pallas_call(
        functools.partial(body, rows_n, cols_n, plane),
        out_shape=(
            jax.ShapeDtypeStruct((1, n_sim), f32),
            jax.ShapeDtypeStruct((1, n_obs), f32),
            jax.ShapeDtypeStruct((1, 1), f32),
        ),
        in_specs=[vmem] * 4,
        out_specs=(vmem,) * 3,
        scratch_shapes=[
            pltpu.VMEM((plane, depth, n_sim), f32),
            pltpu.VMEM((lines, depth, n_obs), f32),
            pltpu.VMEM((n_j, n_i), f32),
            pltpu.VMEM((PARTS, n_j, n_i), bf16),
            pltpu.VMEM((PARTS, n_j, n_i), bf16),
            pltpu.VMEM((group, 2, n_i), f32),
            pltpu.VMEM((lines, 2, n_j), f32),
            pltpu.VMEM((2, group, 1, n_i), f32),
            pltpu.VMEM((2, lines, 1, n_j), f32),
            pltpu.VMEM((group, 1, 128), f32),
            pltpu.SemaphoreType.DMA((9,)),
            pltpu.SemaphoreType.DMA((9,)),
        ],
        compiler_params=pltpu.CompilerParams(
            collective_id=0, has_side_effects=True, vmem_limit_bytes=48 * 2**20
        ),
        name="sinkhorn",
    )(sim_points, obs_points, sim_logw[None, :], obs_logw[None, :])
    return f[0], g[0], cost[0]


def solution(mesh):
    P = jax.sharding.PartitionSpec
    in_specs = (P(None, "row"), P(None, ("row", "col")), P("row"), P(("row", "col")))
    out_specs = (P("row"), P(("row", "col")), P())
    sizes = (mesh.shape["row"], mesh.shape["col"])
    return jax.shard_map(
        functools.partial(on_device, sizes),
        mesh=mesh, in_specs=in_specs, out_specs=out_specs, check_vma=False,
    )
```

time: 771 us -> 85.5 us (0.11)
  blocking collectives: 741 us -> 0 us
  Pallas kernels: 0 us -> 79.5 us
  other arithmetic: 17 us -> 0 us
    all_gather x34 -> x0, blocking collectives: 704 us -> none  [the longest x32 623 us: joined(): pieces = jax.tree.map(lambda part: lax.all_gather(part, axis), value)]
    pallas_call x0 -> x1, Pallas kernels: none -> 79.5 us  [on_device(): pl.pallas_call(functools.partial(body, rows_n, cols_n, plane), out_shape=...]
    psum x1 -> x0, blocking collectives: 37.1 us -> none  [on_device(): total_cost = lax.psum(jnp.sum(transport * costs_tile), ('row', 'col'))]
    reduce_sum x19 -> x0, other arithmetic: 10.7 us -> none  [the longest x8 4.26 us: on_device(): row_mass = jnp.sum(jnp.exp(scores - row_top[:, None]), 1)]
where the time goes in v1:
time: 85.5 us; the launch traced here: 85.2 us
  Pallas kernels  79.5 us (93%)
  local copies, waits for them, and re-layouts  3.34 us (4%)
  between operations  2.41 us (3%)
    pallas_call x1, Pallas kernels, on_device(): pl.pallas_call(functools.partial(body, rows_n, cols_n, plane), out_shape=...  79.5 us
    unnamed x10, local copies, waits for them, and re-layouts  3.34 us

profile of v1, /device:TPU:0, one launch (start us, length us, event | category | flops | bytes accessed | tf_op | source)
XLA Modules:
  0.0 85.2 jit_solution(28600051726008244)
XLA Ops:
  0.6 0.0 copy-start.2
  0.6 0.0 copy-start.3
  0.7 0.7 copy-done.2
  1.3 0.0 copy-done.3
  1.3 0.0 copy-start
  1.3 0.8 copy-done
  2.2 0.0 copy-start.1
  2.2 0.8 copy-done.1
  2.9 79.5 %sinkhorn.1 = (f32[1,256]{1,0:T(1,128)S(1)}, f32[1,128]{1,0:T(1,128)S(1)}, f32[1,1]{1,0:T(1,128)}) custom-call(f32[64,256]{1,0:T(8,128)S(1)} %copy-done, f32[64,128]{1,0:T(8,128)S(1)} %copy-done.1, f32[1,256]{1,0:T(1,128)S(1)} %bitcast.5, f32[1,128]{1,0:T(1,128)S(1)} %bitcast.7), custom_call_target="tpu_custom_call" | custom-call | tf_op jit(solution)/shard_map/sinkhorn/pallas_call | solution.py:275
  82.4 0.6 copy.10
  83.0 0.5 copy.11
Async XLA Ops:
  0.6 0.7 copy-start.2
  0.6 0.7 copy-start.3
  1.3 0.8 copy-start
  2.2 0.8 copy-start.1

commit v2 on v1

--- a/solution.py
+++ b/solution.py
@@ -54,8 +54,8 @@
 def body(
     rows_n, cols_n, plane,
     sim_ref, obs_ref, slw_ref, olw_ref,
-    f_ref, g_ref, cost_ref,
-    simg, obsg, d_ref, k_ref, x_ref,
+    out_ref,
+    slw_buf, olw_buf, load_sem, simg, obsg, d_ref, k_ref, x_ref,
     row_first, col_first, row_buf, col_buf, end_buf,
     send_sem, recv_sem,
 ):
@@ -82,13 +82,23 @@
     for step in range(1, plane):
         core_peers.append((z * plane + (q + step) % plane, c))
 
+    loads = [
+        pltpu.make_async_copy(sim_ref, simg.at[q, pl.ds(0, width)], load_sem.at[0]),
+        pltpu.make_async_copy(obs_ref, obsg.at[z, pl.ds(0, width)], load_sem.at[1]),
+        pltpu.make_async_copy(slw_ref, slw_buf, load_sem.at[2]),
+        pltpu.make_async_copy(olw_ref, olw_buf, load_sem.at[3]),
+    ]
+    for load in loads:
+        load.start()
     barrier = pltpu.get_barrier_semaphore()
     for peer in plane_peers + line_peers:
         pl.semaphore_signal(barrier, inc=1, device_id=peer, device_id_type=MESH)
 
     scale = LOG2E / (EPSILON * width)
-    x = sim_ref[...]
-    y = obs_ref[...]
+    for load in loads:
+        load.wait()
+    x = simg[q, :width, :]
+    y = obsg[z, :width, :]
     pad = simg.shape[1] - width
 
     def tail(values, n):
@@ -100,14 +110,12 @@
         return out
 
     one = jnp.ones((1, n_sim), jnp.float32)
-    simg[q, :width, :] = x
     simg[q, width:, :] = tail(
-        [jnp.sum(x * x, 0, keepdims=True), one, slw_ref[...]], n_sim
+        [jnp.sum(x * x, 0, keepdims=True), one, slw_buf[...]], n_sim
     )
-    ones_obs = jnp.full((1, n_obs), scale, jnp.float32)
-    obsg[z, :width, :] = y * (-2.0 * scale)
+    ones_obs = jnp.ones((1, n_obs), jnp.float32)
     obsg[z, width:, :] = tail(
-        [ones_obs, jnp.sum(y * y, 0, keepdims=True) * scale, None, olw_ref[...]], n_obs
+        [ones_obs, jnp.sum(y * y, 0, keepdims=True), None, olw_buf[...]], n_obs
     )
     pl.semaphore_wait(barrier, len(plane_peers) + len(line_peers))
 
@@ -137,8 +145,10 @@
         [obsg[k, width + 3:width + 4, :] for k in range(lines)], axis=1
     ) * LOG2E - math.log2(n_obs * rows_n * cols_n)
 
+    index = lax.broadcasted_iota(jnp.int32, (width + pad, n_obs), 0)
+    factor = jnp.where(index < width, -2.0 * scale, scale)
     for k in range(lines):
-        left = obsg[k].T
+        left = (obsg[k] * factor).T
         for m in range(plane):
             d_ref[k * n_obs:(k + 1) * n_obs, m * n_sim:(m + 1) * n_sim] = lax.dot_general(
                 left, simg[m], (((1,), (0,)), ((), ())),
@@ -175,22 +185,23 @@
     a_lifted = jnp.exp2(log_a + LIFT)
     b_lifted = jnp.exp2(log_b + LIFT)
 
-    def store_parts(ref, value, rows):
+    def store_parts(ref, value, rows, parts):
         high = value.astype(jnp.bfloat16)
         ref[0, rows, :] = high
-        if PARTS > 1:
+        if parts > 1:
             ref[1, rows, :] = (value - high.astype(jnp.float32)).astype(jnp.bfloat16)
 
-    def build(f, g, with_cost):
+    def build(f, g, last):
+        parts = PARTS if last else 1
         column = to_column(g + LIFT)
         for j in range(0, n_j, 64):
             rows = pl.ds(j, 64)
             piece = column[j:j + 64]
             shift = jnp.concatenate([piece] * (n_i // 128), axis=1)
             values = jnp.exp2((f + shift) - d_ref[rows, :])
-            store_parts(k_ref, values, rows)
-            if with_cost:
-                store_parts(x_ref, values * d_ref[rows, :], rows)
+            store_parts(k_ref, values, rows, parts)
+            if last:
+                store_parts(x_ref, values * d_ref[rows, :], rows, 1)
 
     def total_of(buf, count):
         total = buf[0, 0:1, :]
@@ -198,16 +209,16 @@
             total = total + buf[k, 0:1, :]
         return total
 
-    def row_half(v_rows, parity):
+    def row_half(v_rows, parity, parts):
         buf = row_buf.at[parity]
-        buf[me, 0:1, :] = matvec(v_rows, [k_ref.at[p] for p in range(PARTS)], 0)
+        buf[me, 0:1, :] = matvec(v_rows, [k_ref.at[p] for p in range(parts)], 0)
         exchange(buf, me, plane_peers, 4 + parity)
         finish(buf, plane_peers, 4 + parity)
         return a_lifted / total_of(buf, group)
 
     def col_half(u, parity):
         buf = col_buf.at[parity]
-        buf[z, 0:1, :] = matvec(split_rows(u), [k_ref.at[p] for p in range(PARTS)], 1)
+        buf[z, 0:1, :] = matvec(split_rows(u), [k_ref.at[0]], 1)
         exchange(buf, z, line_peers, 6 + parity)
         finish(buf, line_peers, 6 + parity)
         return b_lifted / total_of(buf, lines)
@@ -220,7 +231,7 @@
         def step(iteration, carry):
             _, v = carry
             parity = iteration % 2
-            u = row_half(split_rows(v), parity)
+            u = row_half(split_rows(v), parity, 1)
             return u, col_half(u, parity)
 
         u, v = lax.fori_loop(
@@ -233,16 +244,16 @@
 
     build(f, g, True)
     parity = (ITERS - 1) % 2
-    u = row_half(split_rows(jnp.ones((1, n_j), jnp.float32)), parity)
+    u = row_half(split_rows(jnp.ones((1, n_j), jnp.float32)), parity, PARTS)
     u_rows = split_rows(u)
     col_first[z, 0:1, :] = matvec(u_rows, [k_ref.at[p] for p in range(PARTS)], 1)
-    col_first[z, 1:2, :] = matvec(u_rows, [x_ref.at[p] for p in range(PARTS)], 1)
+    col_first[z, 1:2, :] = matvec(u_rows, [x_ref.at[0]], 1)
     exchange(col_first, z, line_peers, 3)
     f = f + jnp.log2(u)
     f_mine = f[:, 0:n_sim]
     for k in range(1, plane):
         f_mine = jnp.where(q == k, f[:, k * n_sim:(k + 1) * n_sim], f_mine)
-    f_ref[...] = f_mine * (EPSILON / LOG2E)
+    out_ref[:, 0:n_sim] = f_mine * (EPSILON / LOG2E)
     finish(col_first, line_peers, 3)
     sums = col_first[0]
     for k in range(1, lines):
@@ -255,9 +266,9 @@
     g_mine = g[:, 0:n_obs]
     for k in range(1, lines):
         g_mine = jnp.where(z == k, g[:, k * n_obs:(k + 1) * n_obs], g_mine)
-    g_ref[...] = g_mine * (EPSILON / LOG2E)
+    out_ref[:, n_sim:n_sim + n_obs] = g_mine * (EPSILON / LOG2E)
     finish(end_buf, plane_peers, 8)
-    cost_ref[...] = total_of(end_buf, group)[:, 0:1]
+    out_ref[:, n_sim + n_obs:] = total_of(end_buf, group)
 
 
 def on_device(sizes, sim_points, obs_points, sim_logw, obs_logw):
@@ -272,21 +283,20 @@
     depth = -(-width // 8) * 8 + 8
     assert width % 8 == 0
     vmem = pl.BlockSpec(memory_space=pltpu.VMEM)
-    f, g, cost = pl.pallas_call(
+    out = pl.pallas_call(
         functools.partial(body, rows_n, cols_n, plane),
-        out_shape=(
-            jax.ShapeDtypeStruct((1, n_sim), f32),
-            jax.ShapeDtypeStruct((1, n_obs), f32),
-            jax.ShapeDtypeStruct((1, 1), f32),
-        ),
-        in_specs=[vmem] * 4,
-        out_specs=(vmem,) * 3,
+        out_shape=jax.ShapeDtypeStruct((1, n_sim + n_obs + 128), f32),
+        in_specs=[pl.BlockSpec(memory_space=pltpu.HBM)] * 4,
+        out_specs=vmem,
         scratch_shapes=[
+            pltpu.VMEM((1, n_sim), f32),
+            pltpu.VMEM((1, n_obs), f32),
+            pltpu.SemaphoreType.DMA((4,)),
             pltpu.VMEM((plane, depth, n_sim), f32),
             pltpu.VMEM((lines, depth, n_obs), f32),
             pltpu.VMEM((n_j, n_i), f32),
             pltpu.VMEM((PARTS, n_j, n_i), bf16),
-            pltpu.VMEM((PARTS, n_j, n_i), bf16),
+            pltpu.VMEM((1, n_j, n_i), bf16),
             pltpu.VMEM((group, 2, n_i), f32),
             pltpu.VMEM((lines, 2, n_j), f32),
             pltpu.VMEM((2, group, 1, n_i), f32),
@@ -296,11 +306,12 @@
             pltpu.SemaphoreType.DMA((9,)),
         ],
         compiler_params=pltpu.CompilerParams(
-            collective_id=0, has_side_effects=True, vmem_limit_bytes=48 * 2**20
+            collective_id=0, has_side_effects=True, vmem_limit_bytes=57 * 2**20
         ),
         name="sinkhorn",
     )(sim_points, obs_points, sim_logw[None, :], obs_logw[None, :])
-    return f[0], g[0], cost[0]
+    out = out[0]
+    return out[:n_sim], out[n_sim:n_sim + n_obs], out[n_sim + n_obs:n_sim + n_obs + 1]
 
 
 def solution(mesh):

time: 85.5 us -> 79.6 us (0.931)
  Pallas kernels: 79.5 us -> 76.6 us
  between operations: 2.41 us -> 0.65 us
  local copies, waits for them, and re-layouts: 3.34 us -> 2.26 us
    unnamed x10 -> x2, local copies, waits for them, and re-layouts: 3.34 us -> 0.01 us
    pallas_call x1, Pallas kernels: 79.5 us -> 76.6 us  [on_device(): pl.pallas_call(functools.partial(body, rows_n, cols_n, plane), out_shape=...]
    slice x0 -> x3, local copies, waits for them, and re-layouts: none -> 2.26 us  [the longest x1 1.18 us: on_device(): out[n_sim + n_obs:n_sim + n_obs + 1]]
where the time goes in v2:
time: 79.6 us; the launch traced here: 79.5 us
  Pallas kernels  76.6 us (96%)
  local copies, waits for them, and re-layouts  2.26 us (3%)
    pallas_call x1, Pallas kernels, on_device(): pl.pallas_call(functools.partial(body, rows_n, cols_n, plane), out_shape=...  76.6 us

profile of v2, /device:TPU:0, one launch (start us, length us, event | category | flops | bytes accessed | tf_op | source)
XLA Modules:
  0.0 79.5 jit_solution(3207420246673928621)
XLA Ops:
  0.6 76.6 %sinkhorn.1 = f32[1,512]{1,0:T(1,128)} custom-call(f32[64,256]{1,0:T(8,128)} %sim_ref.1, f32[64,128]{1,0:T(8,128)} %obs_ref.1, f32[1,256]{1,0:T(1,128)} %bitcast.6, f32[1,128]{1,0:T(1,128)} %bitcast.8), custom_call_target="tpu_custom_call" | custom-call | tf_op jit(solution)/shard_map/sinkhorn/pallas_call | solution.py:286
  77.2 0.0 copy-start
  77.2 1.2 %slice.22 = f32[1,1]{1,0:T(1,128)} slice(f32[1,512]{1,0:T(1,128)} %sinkhorn.1), slice={[0:1], [384:385]} | slice | bytes 8 | tf_op jit(solution)/shard_map/slice | solution.py:314
  78.4 0.0 copy-done
  78.4 0.5 slice_bitcast_fusion
  78.9 0.6 slice.18
Async XLA Ops:
  77.2 1.2 %copy-start = (f32[1,512]{1,0:T(1,128)S(1)}, f32[1,512]{1,0:T(1,128)}, u32[]{:S(2)}) copy-start(f32[1,512]{1,0:T(1,128)} %sinkhorn.1) | copy-start | bytes 6148

commit v3 on v2

--- a/solution.py
+++ b/solution.py
@@ -11,7 +11,7 @@
 EPSILON = 0.05
 LOG2E = 1.0 / math.log(2.0)
 PLANE = 4
-REBUILD = 3
+REBUILD = 2
 LIFT = 60.0
 MESH = pl.DeviceIdType.MESH
 PARTS = 2
@@ -136,6 +136,9 @@
     exchange(obsg, z, line_peers, 0)
     exchange(simg, q, core_peers, 1)
     finish(obsg, line_peers, 0)
+    index = lax.broadcasted_iota(jnp.int32, (width + pad, n_obs), 0)
+    factor = jnp.where(index < width, -2.0 * scale, scale)
+    lefts = [(obsg[k] * factor).T for k in range(lines)]
     finish(simg, core_peers, 1)
 
     log_a = jnp.concatenate(
@@ -145,10 +148,8 @@
         [obsg[k, width + 3:width + 4, :] for k in range(lines)], axis=1
     ) * LOG2E - math.log2(n_obs * rows_n * cols_n)
 
-    index = lax.broadcasted_iota(jnp.int32, (width + pad, n_obs), 0)
-    factor = jnp.where(index < width, -2.0 * scale, scale)
     for k in range(lines):
-        left = (obsg[k] * factor).T
+        left = lefts[k]
         for m in range(plane):
             d_ref[k * n_obs:(k + 1) * n_obs, m * n_sim:(m + 1) * n_sim] = lax.dot_general(
                 left, simg[m], (((1,), (0,)), ((), ())),
@@ -216,35 +217,38 @@
         finish(buf, plane_peers, 4 + parity)
         return a_lifted / total_of(buf, group)
 
-    def col_half(u, parity):
+    def col_start(u, parity):
         buf = col_buf.at[parity]
         buf[z, 0:1, :] = matvec(split_rows(u), [k_ref.at[0]], 1)
         exchange(buf, z, line_peers, 6 + parity)
+
+    def col_finish(parity):
+        buf = col_buf.at[parity]
         finish(buf, line_peers, 6 + parity)
         return b_lifted / total_of(buf, lines)
 
-    done = 1
-    while done < ITERS - 1:
-        count = min(REBUILD, ITERS - 1 - done)
-        build(f, g, False)
-
-        def step(iteration, carry):
-            _, v = carry
-            parity = iteration % 2
+    def block(first, f, g, v, last):
+        for k in range(REBUILD):
+            parity = (first + k) % 2
             u = row_half(split_rows(v), parity, 1)
-            return u, col_half(u, parity)
-
-        u, v = lax.fori_loop(
-            done, done + count, step,
-            (jnp.ones((1, n_i), jnp.float32), jnp.ones((1, n_j), jnp.float32)),
-        )
+            col_start(u, parity)
+            if k < REBUILD - 1:
+                v = col_finish(parity)
         f = f + jnp.log2(u)
         g = g + jnp.log2(v)
-        done += count
-
-    build(f, g, True)
-    parity = (ITERS - 1) % 2
-    u = row_half(split_rows(jnp.ones((1, n_j), jnp.float32)), parity, PARTS)
+        build(f, g, last)
+        return f, g, col_finish(parity) / v
+
+    blocks = (ITERS - 2) // REBUILD
+    assert blocks * REBUILD == ITERS - 2 and REBUILD % 2 == 0
+    build(f, g, False)
+    f, g, v = lax.fori_loop(
+        0, blocks - 1, lambda k, carry: block(1, *carry, False),
+        (f, g, jnp.ones((1, n_j), jnp.float32)),
+    )
+    f, g, v = block(1, f, g, v, True)
+
+    u = row_half(split_rows(v), (ITERS - 1) % 2, PARTS)
     u_rows = split_rows(u)
     col_first[z, 0:1, :] = matvec(u_rows, [k_ref.at[p] for p in range(PARTS)], 1)
     col_first[z, 1:2, :] = matvec(u_rows, [x_ref.at[0]], 1)

time: 79.6 us -> 78.6 us (0.987)
  Pallas kernels: 76.6 us -> 75.5 us
    pallas_call x1, Pallas kernels: 76.6 us -> 75.5 us  [on_device(): pl.pallas_call(functools.partial(body, rows_n, cols_n, plane), out_shape=...]
where the time goes in v3:
time: 78.6 us; the launch traced here: 78.5 us
  Pallas kernels  75.5 us (96%)
  local copies, waits for them, and re-layouts  2.26 us (3%)
    pallas_call x1, Pallas kernels, on_device(): pl.pallas_call(functools.partial(body, rows_n, cols_n, plane), out_shape=...  75.5 us

profile of v3, /device:TPU:0, one launch (start us, length us, event | category | flops | bytes accessed | tf_op | source)
XLA Modules:
  0.0 78.5 jit_solution(11070256810118553632)
XLA Ops:
  0.6 75.5 %sinkhorn.1 = f32[1,512]{1,0:T(1,128)} custom-call(f32[64,256]{1,0:T(8,128)} %sim_ref.1, f32[64,128]{1,0:T(8,128)} %obs_ref.1, f32[1,256]{1,0:T(1,128)} %bitcast.6, f32[1,128]{1,0:T(1,128)} %bitcast.8), custom_call_target="tpu_custom_call" | custom-call | tf_op jit(solution)/shard_map/sinkhorn/pallas_call | solution.py:290
  76.2 0.0 copy-start
  76.2 1.2 %slice.22 = f32[1,1]{1,0:T(1,128)} slice(f32[1,512]{1,0:T(1,128)} %sinkhorn.1), slice={[0:1], [384:385]} | slice | bytes 8 | tf_op jit(solution)/shard_map/slice | solution.py:318
  77.4 0.0 copy-done
  77.4 0.5 slice_bitcast_fusion
  77.9 0.6 slice.18
Async XLA Ops:
  76.2 1.2 %copy-start = (f32[1,512]{1,0:T(1,128)S(1)}, f32[1,512]{1,0:T(1,128)}, u32[]{:S(2)}) copy-start(f32[1,512]{1,0:T(1,128)} %sinkhorn.1) | copy-start | bytes 6148

commit v4 on v3

--- a/solution.py
+++ b/solution.py
@@ -133,8 +133,8 @@
             pltpu.make_async_copy(some, some, recv_sem.at[sem]).wait()
             pltpu.make_async_copy(some, some, send_sem.at[sem]).wait()
 
+    exchange(simg, q, core_peers, 1)
     exchange(obsg, z, line_peers, 0)
-    exchange(simg, q, core_peers, 1)
     finish(obsg, line_peers, 0)
     index = lax.broadcasted_iota(jnp.int32, (width + pad, n_obs), 0)
     factor = jnp.where(index < width, -2.0 * scale, scale)
@@ -180,11 +180,10 @@
     col_first[z, 0:1, :] = to_row(low)
     col_first[z, 1:2, :] = to_row(mass)
     exchange(col_first, z, line_peers, 3)
+    a_lifted = jnp.exp2(log_a + LIFT)
+    b_lifted = jnp.exp2(log_b + LIFT)
     finish(col_first, line_peers, 3)
     g = log_b + merge(col_first, lines)
-
-    a_lifted = jnp.exp2(log_a + LIFT)
-    b_lifted = jnp.exp2(log_b + LIFT)
 
     def store_parts(ref, value, rows, parts):
         high = value.astype(jnp.bfloat16)

time: 78.6 us -> 78.6 us (level)
  no operation moved by 1% of the time
where the time goes in v4:
time: 78.6 us; the launch traced here: 78.5 us
  Pallas kernels  75.5 us (96%)
  local copies, waits for them, and re-layouts  2.26 us (3%)
    pallas_call x1, Pallas kernels, on_device(): pl.pallas_call(functools.partial(body, rows_n, cols_n, plane), out_shape=...  75.5 us

profile of v4, /device:TPU:0, one launch (start us, length us, event | category | flops | bytes accessed | tf_op | source)
XLA Modules:
  0.0 78.5 jit_solution(3074357423004592692)
XLA Ops:
  0.6 75.5 %sinkhorn.1 = f32[1,512]{1,0:T(1,128)} custom-call(f32[64,256]{1,0:T(8,128)} %sim_ref.1, f32[64,128]{1,0:T(8,128)} %obs_ref.1, f32[1,256]{1,0:T(1,128)} %bitcast.6, f32[1,128]{1,0:T(1,128)} %bitcast.8), custom_call_target="tpu_custom_call" | custom-call | tf_op jit(solution)/shard_map/sinkhorn/pallas_call | solution.py:289
  76.2 0.0 copy-start
  76.2 1.2 %slice.22 = f32[1,1]{1,0:T(1,128)} slice(f32[1,512]{1,0:T(1,128)} %sinkhorn.1), slice={[0:1], [384:385]} | slice | bytes 8 | tf_op jit(solution)/shard_map/slice | solution.py:317
  77.4 0.0 copy-done
  77.4 0.5 slice_bitcast_fusion
  77.9 0.6 slice.18
Async XLA Ops:
  76.2 1.2 %copy-start = (f32[1,512]{1,0:T(1,128)S(1)}, f32[1,512]{1,0:T(1,128)}, u32[]{:S(2)}) copy-start(f32[1,512]{1,0:T(1,128)} %sinkhorn.1) | copy-start | bytes 6148
